TPU v7x, 512 devices: a whole 4x8x8 slice. The times are simulated.
512 devices in a mesh: dp: 64 (over x, y, core), code: 8 (over z).
Axes of the slice: x: 4, y: 8, z: 8, core: 2. Of those that a mesh axis runs over, the one named last changes fastest.
Arguments:
- items: float32 [65536, 512], P(('dp', 'code')), may hold values from -6 to 6
- codewords: float32 [8192, 512], P('code'), may hold values from -6 to 6
- assign: int32 [65536], P('dp'), may hold values from 0 to 8191, as said below
Outputs:
- new_codewords: float32 [8192, 512], P('code', 'dp')
- residual: float32 [65536, 512], P(('dp', 'code'))
Inputs may be any that keep to these rules, and one draw needn't show every extreme that they name: `assign`: the items are laid out in aligned blocks of 128 (the items of one device). Splitting the codewords into equal ranges, one per index of code, the items of one block name codewords of exactly half of the ranges, 32 items for each such range.
All inputs are finite; a program needn't handle non-finite values.
Results may differ from a plain program's by a relative error of at most 0.0003.
Values sent between devices are 32-bit elements; how exact they have to be, the bound alone decides.
No kernel may reach another device: no remote copies, remote signals or barrier semaphores. Data moves between devices by JAX's collectives and lax.ppermute only.
A program may use at most 64 MiB of HBM per device.

v0:
```python
import jax
import jax.numpy as jnp
from jax import lax
from jax.sharding import PartitionSpec as P

K = 8192
ITERS = 3
epsilon = 1e-05
inverse_temp = 64.0


def unit_rows(values):
    return values * lax.rsqrt(jnp.mean(values * values, axis=-1, keepdims=True) + epsilon)


def kernel_of(rows_block, scaled):
    return jnp.exp(
        jnp.dot(
            unit_rows(rows_block),
            scaled.T,
            precision=lax.Precision.HIGHEST,
            preferred_element_type=jnp.float32,
        )
    )


def column_scale(col_part):
    summed = lax.psum(col_part, "dp")
    return 1.0 / (K * summed)


def row_scaling(row_part, total_items):
    summed = lax.psum(row_part, "code")
    return 1.0 / (total_items * summed)


def body(items, codewords, assign):
    code_count = lax.axis_size("code")
    dp_count = lax.axis_size("dp")
    local_codes = codewords.shape[0]
    width = items.shape[1]
    own_rows = items.shape[0]
    total_items = own_rows * code_count * dp_count
    scaled = unit_rows(codewords) * (inverse_temp / width)
    gathered = lax.all_gather(items, "code", axis=0, tiled=True)
    kernel_vals = kernel_of(gathered, scaled)
    col_part = jnp.sum(kernel_vals, axis=0)
    row_scale = jnp.ones((kernel_vals.shape[0],), jnp.float32)
    for sweep_index in range(ITERS):
        col_scale = column_scale(col_part)
        row_part = jnp.dot(
            kernel_vals,
            col_scale,
            precision=lax.Precision.HIGHEST,
            preferred_element_type=jnp.float32,
        )
        row_scale = row_scaling(row_part, total_items)
        col_part = jnp.dot(
            row_scale,
            kernel_vals,
            precision=lax.Precision.HIGHEST,
            preferred_element_type=jnp.float32,
        )
    mass = lax.psum(col_part, "dp")
    numerator = lax.dot_general(
        kernel_vals,
        row_scale[:, None] * gathered,
        (((0,), (0,)), ((), ())),
        precision=lax.Precision.HIGHEST,
        preferred_element_type=jnp.float32,
    )
    owned_sums = lax.psum_scatter(numerator, "dp", scatter_dimension=1, tiled=True)
    new_codewords = owned_sums / mass[:, None]
    my_code = lax.axis_index("code")
    offset = my_code * local_codes
    index_rows = assign - offset
    inside = (index_rows >= 0) & (index_rows < local_codes)
    picked = jnp.take(codewords, jnp.clip(index_rows, 0, local_codes - 1), axis=0)
    looked = lax.psum_scatter(
        jnp.where(inside[:, None], picked, jnp.float32(0.0)),
        "code",
        scatter_dimension=0,
        tiled=True,
    )
    residual = items - looked
    return (new_codewords, residual)


def solution(mesh):
    in_specs = (P(("dp", "code"), None), P("code", None), P("dp"))
    out_specs = (P("code", "dp"), P(("dp", "code"), None))
    return jax.shard_map(body, mesh=mesh, in_specs=in_specs, out_specs=out_specs, check_vma=False)
```

profile of v0, /device:TPU:16, one launch (start us, length us, event | category | flops | bytes accessed | tf_op | source)
XLA Modules:
  0.0 675.3 jit_solution(14707872022729318664)
XLA Ops:
  7.2 0.0 all-gather.2.cloned.1.call-start
  7.2 0.7 all-gather.2.cloned.1.call-update
  7.9 0.0 reduce-scatter.5.cloned.1.call-start
  7.9 0.7 fusion.23
  8.6 0.0 copy-start.4
  8.6 5.6 gather_fusion
  14.3 0.0 copy-done.4
  14.3 2.0 select_select_fusion
  16.3 0.0 copy-start
  16.3 0.0 reduce-scatter.5.cloned.1.call-update
  16.3 0.0 reduce-scatter.3.cloned.1.call-start
  16.4 1.5 copy-done
  17.9 0.2 multiply_reduce_fusion
  18.1 41.1 %all-gather.2.cloned.1.call-done = f32[1024,512]{1,0:T(8,128)} async-done(((f32[128,512]{1,0:T(8,128)}), f32[1024,512]{1,0:T(8,128)}) %all-gather.2.cloned.1.call-update) | async-done | bytes 2097168 | tf_op jit(solution)/shard_map/all_gather | solution.py:45
  59.2 0.0 copy-start.1
  59.2 2.0 multiply_reduce_fusion.1
  61.2 0.3 copy-done.1
  61.5 9.1 %exponential_reduce_fusion = (f32[1024]{0:T(1024)S(1)}, f32[1024,1024]{1,0:T(8,128)}) fusion(f32[1024,512]{1,0:T(8,128)S(1)} %copy-done, f32[1024]{0:T(1024)S(1)} %add_rsqrt_fusion, f32[1024,512]{1,0:T(8,128)S(1)} %copy-done.1, f32[1024]{0:T(1024)S(1)} %add_rsqrt_fusion.1), kind=kOutput, calls=%fused_computation.15 | convolution fusion | flops 6445071360 | bytes 8400896 | tf_op jit(solution)/shard_map/dot_general | solution.py:18
  70.5 114.3 %psum.49 = f32[1024]{0:T(1024)S(1)} all-reduce(f32[1024]{0:T(1024)S(1)} %get-tuple-element.4), channel_id=1, replica_groups=mesh['dp'=64,'code'=8] {'dp'}, use_global_device_ids=true, to_apply=%region_3.0 | all-reduce | flops 1024 | bytes 8192 | tf_op jit(solution)/shard_map/psum | solution.py:28
  184.8 6.2 fusion.12
  191.0 16.1 %psum.50 = f32[1024]{0:T(1024)S(1)} all-reduce(f32[1024]{0:T(1024)S(1)} %bitcast.21), channel_id=1, replica_groups=mesh['dp'=64,'code'=8] {'code'}, use_global_device_ids=true, to_apply=%region_4.0 | all-reduce | flops 1024 | bytes 8192 | tf_op jit(solution)/shard_map/psum | solution.py:33
  207.1 4.5 fusion.10
  211.6 124.2 %psum.51 = f32[1024]{0:T(1024)S(1)} all-reduce(f32[1024]{0:T(1024)S(1)} %bitcast.23), channel_id=1, replica_groups=mesh['dp'=64,'code'=8] {'dp'}, use_global_device_ids=true, to_apply=%region_5.0 | all-reduce | flops 1024 | bytes 8192 | tf_op jit(solution)/shard_map/psum | solution.py:28
  335.8 6.2 fusion.8
  342.0 14.2 %psum.52 = f32[1024]{0:T(1024)S(1)} all-reduce(f32[1024]{0:T(1024)S(1)} %bitcast.25), channel_id=1, replica_groups=mesh['dp'=64,'code'=8] {'code'}, use_global_device_ids=true, to_apply=%region_6.0 | all-reduce | flops 1024 | bytes 8192 | tf_op jit(solution)/shard_map/psum | solution.py:33
  356.2 4.5 fusion.6
  360.7 124.0 %psum.53 = f32[1024]{0:T(1024)S(1)} all-reduce(f32[1024]{0:T(1024)S(1)} %bitcast.27), channel_id=1, replica_groups=mesh['dp'=64,'code'=8] {'dp'}, use_global_device_ids=true, to_apply=%region_7.0 | all-reduce | flops 1024 | bytes 8192 | tf_op jit(solution)/shard_map/psum | solution.py:28
  484.7 0.0 copy-start.2
  484.7 6.3 fusion.4
  491.1 16.4 %psum.54 = f32[1024]{0:T(1024)S(1)} all-reduce(f32[1024]{0:T(1024)S(1)} %bitcast.29), channel_id=1, replica_groups=mesh['dp'=64,'code'=8] {'code'}, use_global_device_ids=true, to_apply=%region_8.0 | all-reduce | flops 1024 | bytes 8192 | tf_op jit(solution)/shard_map/psum | solution.py:33
  507.4 0.0 copy-done.2
  507.5 10.3 %fusion.2 = f32[1024,512]{0,1:T(8,128)} fusion(f32[1024,1024]{1,0:T(8,128)} %get-tuple-element.5, f32[1024,512]{1,0:T(8,128)S(1)} %copy-done.2, f32[1024]{0:T(1024)S(1)} %multiply_divide_fusion), kind=kOutput, calls=%fused_computation.3 | convolution fusion | flops 6442975232 | bytes 8392704 | tf_op jit(solution)/shard_map/dot_general | solution.py:65
  517.8 0.0 reduce-scatter.3.cloned.1.call-update
  517.8 0.0 copy-start.3
  517.8 4.5 fusion
  522.4 124.2 %psum.55 = f32[1024]{0:T(1024)S(1)} all-reduce(f32[1024]{0:T(1024)S(1)} %bitcast.20), channel_id=1, replica_groups=mesh['dp'=64,'code'=8] {'dp'}, use_global_device_ids=true, to_apply=%region_10.0 | all-reduce | flops 1024 | bytes 8192 | tf_op jit(solution)/shard_map/psum | solution.py:64
  646.6 0.0 reduce-scatter.5.cloned.1.call-done
  646.6 0.0 copy-done.3
  646.6 1.7 sub.11
  648.3 19.1 %reduce-scatter.3.cloned.1.call-done = f32[1024,8]{0,1:T(8,128)} async-done(((f32[1024,512]{0,1:T(8,128)}), f32[1024,8]{0,1:T(8,128)}) %reduce-scatter.3.cloned.1.call-update) | async-done | bytes 32784 | tf_op jit(solution)/shard_map/reduce_scatter | solution.py:72
  667.4 1.4 broadcast_divide_fusion
  (9 shorter events, 0.1 us)
Async XLA Ops:
  7.2 52.1 %all-gather.2.cloned.1.call-start = ((), (), s32[]{:S(2)}) async-start(), calls=%async_computation.2 | async-start | bytes 2359296 | tf_op jit(solution)/shard_map/all_gather | solution.py:45
  7.9 638.7 %reduce-scatter.5.cloned.1.call-start = ((), (), s32[]{:S(2)}) async-start(), calls=%async_computation.4 | async-start | bytes 2359296 | tf_op jit(solution)/shard_map/reduce_scatter | solution.py:79
  8.6 5.6 copy-start.4
  16.3 1.6 copy-start
  16.3 651.1 %reduce-scatter.3.cloned.1.call-start = ((), (), s32[]{:S(2)}) async-start(), calls=%async_computation.3 | async-start | bytes 2129920 | tf_op jit(solution)/shard_map/reduce_scatter | solution.py:72
  59.2 2.2 copy-start.1
  484.7 22.7 %copy-start.2 = (f32[1024,512]{1,0:T(8,128)S(1)}, f32[1024,512]{1,0:T(8,128)}, u32[]{:S(2)}) copy-start(f32[1024,512]{1,0:T(8,128)} %all-gather.2.cloned.1.call-done) | copy-start | bytes 6291460
  517.8 128.8 %copy-start.3 = (f32[128,512]{1,0:T(8,128)S(1)}, f32[128,512]{1,0:T(8,128)}, u32[]{:S(2)}) copy-start(f32[128,512]{1,0:T(8,128)} %param.3) | copy-start | bytes 786436
Sparse Core Ops, SparseCore 0:
  10.1 49.1 all-gather.1
  62.1 43.7 reduce-scatter.4
  517.9 149.3 reduce-scatter.2
where the time goes:
time: 676 us; the launch traced here: 675 us
  blocking collectives  533 us (79%)
  waiting for transfers between devices  60.9 us (9%)
  matrix products  51.6 us (8%)
  between operations  13.9 us (2%)
  other arithmetic  7.99 us (1%)
  local copies, waits for them, and re-layouts  7.4 us (1%)
    psum x3, blocking collectives, column_scale(): summed = lax.psum(col_part, 'dp')  363 us
    psum x1, blocking collectives, body(): mass = lax.psum(col_part, 'dp')  124 us
    psum x3, blocking collectives, row_scaling(): summed = lax.psum(row_part, 'code')  46.7 us
    all_gather x1, waiting for transfers between devices, body(): gathered = lax.all_gather(items, 'code', axis=0, tiled=True)  41.1 us
    reduce_scatter x1, waiting for transfers between devices, body(): lax.psum_scatter(numerator, 'dp', scatter_dimension=1, tiled=True)  19.1 us
    dot_general x3, matrix products, body(): jnp.dot(kernel_vals, col_scale, precision=lax.Precision.HIGHEST, preferre...  18.7 us
  transfers between devices with their start and end apart: 3, of which 2 were waited for; matrix products, arithmetic and copies ran while one was open for 9% of the time, Pallas kernels for 0%

commit v1 on v0

--- a/solution.py
+++ b/solution.py
@@ -7,6 +7,19 @@
 ITERS = 3
 epsilon = 1e-05
 inverse_temp = 64.0
+
+
+def refer_group(vector):
+    windows = [vector]
+    nodes = jax.lax.psum(1, "code")
+    for k in tuple(range(nodes - 1)):
+        y_new = jax.lax.ppermute(
+            windows[-1], "code", [(idx, (idx + 1) % nodes) for idx in range(nodes)]
+        )
+        windows.append(y_new)
+    mid_arr = jnp.concatenate(windows[::-1], axis=0)
+    res = jax.lax.axis_index("code")
+    return jnp.roll(mid_arr, (res + 1) * vector.shape[0], axis=0)
 
 
 def unit_rows(values):
@@ -42,7 +55,7 @@
     own_rows = items.shape[0]
     total_items = own_rows * code_count * dp_count
     scaled = unit_rows(codewords) * (inverse_temp / width)
-    gathered = lax.all_gather(items, "code", axis=0, tiled=True)
+    gathered = refer_group(items)
     kernel_vals = kernel_of(gathered, scaled)
     col_part = jnp.sum(kernel_vals, axis=0)
     row_scale = jnp.ones((kernel_vals.shape[0],), jnp.float32)

time: 676 us -> 741 us (1.096)
  waiting for transfers between devices: 60.9 us -> 94.1 us
  starting transfers between devices: 0.12 us -> 15.8 us
  local copies, waits for them, and re-layouts: 7.4 us -> 21.6 us
    ppermute x0 -> x7, waiting for transfers between devices: none -> 72.6 us  [refer_group(): jax.lax.ppermute(windows[-1], 'code', [(idx, (idx + 1) % nodes) for idx i...]
    all_gather x1 -> x0, waiting for transfers between devices: 41.1 us -> none  [body(): gathered = lax.all_gather(items, 'code', axis=0, tiled=True)]
    ppermute x0 -> x7, starting transfers between devices: none -> 15.7 us  [refer_group(): jax.lax.ppermute(windows[-1], 'code', [(idx, (idx + 1) % nodes) for idx i...]
    unnamed x10 -> x20, local copies, waits for them, and re-layouts: 1.78 us -> 13.9 us
  transfers between devices with their start and end apart: 3 -> 9, of which waited for: 2 -> 8; matrix products, arithmetic and copies ran while one was open for 9% -> 2% of each run, Pallas kernels for 0% -> 0%
where the time goes in v1:
time: 741 us; the launch traced here: 740 us
  blocking collectives  532 us (72%)
  waiting for transfers between devices  94.1 us (13%)
  matrix products  52.9 us (7%)
  local copies, waits for them, and re-layouts  21.6 us (3%)
  starting transfers between devices  15.8 us (2%)
  between operations  14.2 us (2%)
  other arithmetic  10.1 us (1%)
    psum x3, blocking collectives, column_scale(): summed = lax.psum(col_part, 'dp')  363 us
    psum x1, blocking collectives, body(): mass = lax.psum(col_part, 'dp')  124 us
    ppermute x7, waiting for transfers between devices, refer_group(): jax.lax.ppermute(windows[-1], 'code', [(idx, (idx + 1) % nodes) for idx i...  72.6 us
    psum x3, blocking collectives, row_scaling(): summed = lax.psum(row_part, 'code')  44.7 us
    reduce_scatter x1, waiting for transfers between devices, body(): lax.psum_scatter(numerator, 'dp', scatter_dimension=1, tiled=True)  21.4 us
    dot_general x3, matrix products, body(): jnp.dot(kernel_vals, col_scale, precision=lax.Precision.HIGHEST, preferre...  18.5 us
    ppermute x7, starting transfers between devices, refer_group(): jax.lax.ppermute(windows[-1], 'code', [(idx, (idx + 1) % nodes) for idx i...  15.7 us
  transfers between devices with their start and end apart: 9, of which 8 were waited for; matrix products, arithmetic and copies ran while one was open for 2% of the time, Pallas kernels for 0%

profile of v1, /device:TPU:16, one launch (start us, length us, event | category | flops | bytes accessed | tf_op | source)
XLA Modules:
  0.0 740.5 jit_solution(16304761518974999298)
XLA Ops:
  7.2 0.0 reduce-scatter.5.cloned.1.call-start
  7.2 0.7 compare_and_fusion.1
  7.9 0.7 fusion.25
  8.6 6.9 gather_fusion
  15.5 0.0 copy-start.1
  15.5 0.0 copy-start
  15.5 3.3 select_select_fusion
  18.8 0.0 reduce-scatter.5.cloned.1.call-update
  18.9 0.0 reduce-scatter.3.cloned.1.call-start
  18.9 0.0 copy-done.1
  18.9 4.3 collective-permute-start
  23.2 13.0 %collective-permute-done = f32[128,512]{1,0:T(8,128)S(1)} collective-permute-done((f32[128,512]{1,0:T(8,128)S(1)}, f32[128,512]{1,0:T(8,128)S(1)}, u32[]{:S(2)}, u32[]{:S(2)}) %collective-permute-start) | collective-permute-done | bytes 262176 | tf_op jit(solution)/shard_map/ppermute | solution.py:16
  36.2 1.9 collective-permute-start.1
  38.1 14.7 %collective-permute-done.1 = f32[128,512]{1,0:T(8,128)S(1)} collective-permute-done((f32[128,512]{1,0:T(8,128)S(1)}, f32[128,512]{1,0:T(8,128)S(1)}, u32[]{:S(2)}, u32[]{:S(2)}) %collective-permute-start.1) | collective-permute-done | bytes 262176 | tf_op jit(solution)/shard_map/ppermute | solution.py:16
  52.8 1.9 collective-permute-start.2
  54.7 14.4 %collective-permute-done.2 = f32[128,512]{1,0:T(8,128)S(1)} collective-permute-done((f32[128,512]{1,0:T(8,128)S(1)}, f32[128,512]{1,0:T(8,128)S(1)}, u32[]{:S(2)}, u32[]{:S(2)}) %collective-permute-start.2) | collective-permute-done | bytes 262176 | tf_op jit(solution)/shard_map/ppermute | solution.py:16
  69.1 1.9 collective-permute-start.3
  71.0 7.5 %collective-permute-done.3 = f32[128,512]{1,0:T(8,128)S(1)} collective-permute-done((f32[128,512]{1,0:T(8,128)S(1)}, f32[128,512]{1,0:T(8,128)S(1)}, u32[]{:S(2)}, u32[]{:S(2)}) %collective-permute-start.3) | collective-permute-done | bytes 262176 | tf_op jit(solution)/shard_map/ppermute | solution.py:16
  78.6 1.9 collective-permute-start.4
  80.5 7.5 %collective-permute-done.4 = f32[128,512]{1,0:T(8,128)S(1)} collective-permute-done((f32[128,512]{1,0:T(8,128)S(1)}, f32[128,512]{1,0:T(8,128)S(1)}, u32[]{:S(2)}, u32[]{:S(2)}) %collective-permute-start.4) | collective-permute-done | bytes 262176 | tf_op jit(solution)/shard_map/ppermute | solution.py:16
  88.1 1.9 collective-permute-start.5
  90.0 7.8 %collective-permute-done.5 = f32[128,512]{1,0:T(8,128)} collective-permute-done((f32[128,512]{1,0:T(8,128)S(1)}, f32[128,512]{1,0:T(8,128)}, u32[]{:S(2)}, u32[]{:S(2)}) %collective-permute-start.5) | collective-permute-done | bytes 262176 | tf_op jit(solution)/shard_map/ppermute | solution.py:16
  97.8 1.9 collective-permute-start.6
  99.7 0.0 copy-done
  99.7 0.2 multiply_reduce_fusion
  100.0 7.6 %collective-permute-done.6 = f32[128,512]{1,0:T(8,128)} collective-permute-done((f32[128,512]{1,0:T(8,128)}, f32[128,512]{1,0:T(8,128)}, u32[]{:S(2)}, u32[]{:S(2)}) %collective-permute-start.6) | collective-permute-done | bytes 262176 | tf_op jit(solution)/shard_map/ppermute | solution.py:16
  107.6 1.7 constant_dynamic-update-slice_fusion.15
  109.2 1.7 constant_dynamic-update-slice_fusion.14
  110.9 0.7 constant_dynamic-update-slice_fusion.13
  111.6 0.7 constant_dynamic-update-slice_fusion.12
  112.3 0.7 constant_dynamic-update-slice_fusion.11
  113.1 0.7 constant_dynamic-update-slice_fusion.10
  113.8 0.7 constant_dynamic-update-slice_fusion.9
  114.5 0.0 reduce-scatter.5.cloned.1.call-done
  114.5 0.0 copy-start.2
  114.5 1.9 fusion.29
  116.4 1.7 constant_dynamic-update-slice_fusion.7
  118.1 1.7 constant_dynamic-update-slice_fusion.6
  119.8 0.7 constant_dynamic-update-slice_fusion.5
  120.5 0.7 constant_dynamic-update-slice_fusion.4
  121.3 0.7 constant_dynamic-update-slice_fusion.3
  122.0 0.7 constant_dynamic-update-slice_fusion.2
  122.7 0.7 constant_dynamic-update-slice_fusion.1
  123.4 0.0 copy-done.2
  123.4 0.7 constant_dynamic-update-slice_fusion
  124.1 1.8 multiply_reduce_fusion.1
  126.0 10.0 %exponential_reduce_fusion = (f32[1024]{0:T(1024)S(1)}, f32[1024,1024]{1,0:T(8,128)}) fusion(f32[1024,512]{1,0:T(8,128)S(1)} %copy-done, f32[1024]{0:T(1024)S(1)} %add_rsqrt_fusion, f32[2048,512]{1,0:T(8,128)} %constant_dynamic-update-slice_fusion, s32[]{:T(128)S(6)} %select_n.27, f32[1024]{0:T(1024)S(1)} %add_rsqrt_fusion.1), kind=kOutput, calls=%fused_computation.15 | convolution fusion | flops 6445071360 | bytes 8400900 | tf_op jit(solution)/shard_map/dot_general | solution.py:31
  136.0 114.7 %psum.49 = f32[1024]{0:T(1024)S(1)} all-reduce(f32[1024]{0:T(1024)S(1)} %get-tuple-element.6), channel_id=1, replica_groups=mesh['dp'=64,'code'=8] {'dp'}, use_global_device_ids=true, to_apply=%region_3.4 | all-reduce | flops 1024 | bytes 8192 | tf_op jit(solution)/shard_map/psum | solution.py:41
  250.6 6.2 fusion.12
  256.8 14.2 %psum.50 = f32[1024]{0:T(1024)S(1)} all-reduce(f32[1024]{0:T(1024)S(1)} %bitcast.21), channel_id=1, replica_groups=mesh['dp'=64,'code'=8] {'code'}, use_global_device_ids=true, to_apply=%region_4.5 | all-reduce | flops 1024 | bytes 8192 | tf_op jit(solution)/shard_map/psum | solution.py:46
  271.0 4.5 fusion.10
  275.5 124.2 %psum.51 = f32[1024]{0:T(1024)S(1)} all-reduce(f32[1024]{0:T(1024)S(1)} %bitcast.23), channel_id=1, replica_groups=mesh['dp'=64,'code'=8] {'dp'}, use_global_device_ids=true, to_apply=%region_5.6 | all-reduce | flops 1024 | bytes 8192 | tf_op jit(solution)/shard_map/psum | solution.py:41
  399.7 6.2 fusion.8
  405.9 16.2 %psum.52 = f32[1024]{0:T(1024)S(1)} all-reduce(f32[1024]{0:T(1024)S(1)} %bitcast.25), channel_id=1, replica_groups=mesh['dp'=64,'code'=8] {'code'}, use_global_device_ids=true, to_apply=%region_6.7 | all-reduce | flops 1024 | bytes 8192 | tf_op jit(solution)/shard_map/psum | solution.py:46
  422.0 4.5 fusion.6
  426.5 124.0 %psum.53 = f32[1024]{0:T(1024)S(1)} all-reduce(f32[1024]{0:T(1024)S(1)} %bitcast.27), channel_id=1, replica_groups=mesh['dp'=64,'code'=8] {'dp'}, use_global_device_ids=true, to_apply=%region_7.8 | all-reduce | flops 1024 | bytes 8192 | tf_op jit(solution)/shard_map/psum | solution.py:41
  550.6 6.2 fusion.4
  556.7 14.4 %psum.54 = f32[1024]{0:T(1024)S(1)} all-reduce(f32[1024]{0:T(1024)S(1)} %bitcast.29), channel_id=1, replica_groups=mesh['dp'=64,'code'=8] {'code'}, use_global_device_ids=true, to_apply=%region_8.9 | all-reduce | flops 1024 | bytes 8192 | tf_op jit(solution)/shard_map/psum | solution.py:46
  571.1 11.0 %fusion.2 = f32[1024,512]{0,1:T(8,128)} fusion(f32[1024,1024]{1,0:T(8,128)} %get-tuple-element.7, f32[2048,512]{1,0:T(8,128)} %constant_dynamic-update-slice_fusion, s32[]{:T(128)S(6)} %select_n.27, f32[1024]{0:T(1024)S(1)} %multiply_divide_fusion), kind=kOutput, calls=%fused_computation.3 | convolution fusion | flops 6442975232 | bytes 8392708 | tf_op jit(solution)/shard_map/dot_general | solution.py:78
  582.1 0.0 reduce-scatter.3.cloned.1.call-update
  582.1 4.5 fusion
  586.6 124.2 %psum.55 = f32[1024]{0:T(1024)S(1)} all-reduce(f32[1024]{0:T(1024)S(1)} %bitcast.20), channel_id=1, replica_groups=mesh['dp'=64,'code'=8] {'dp'}, use_global_device_ids=true, to_apply=%region_10.11 | all-reduce | flops 1024 | bytes 8192 | tf_op jit(solution)/shard_map/psum | solution.py:77
  710.8 21.4 %reduce-scatter.3.cloned.1.call-done = f32[1024,8]{0,1:T(8,128)} async-done(((f32[1024,512]{0,1:T(8,128)}), f32[1024,8]{0,1:T(8,128)}) %reduce-scatter.3.cloned.1.call-update) | async-done | bytes 32784 | tf_op jit(solution)/shard_map/reduce_scatter | solution.py:85
  732.2 1.4 broadcast_divide_fusion
  (8 shorter events, 0.1 us)
Async XLA Ops:
  7.2 107.4 %reduce-scatter.5.cloned.1.call-start = ((), (), s32[]{:S(2)}) async-start(), calls=%async_computation.3 | async-start | bytes 2359296 | tf_op jit(solution)/shard_map/reduce_scatter | solution.py:92
  15.5 3.4 copy-start.1
  15.5 84.2 %copy-start = (f32[1024,512]{1,0:T(8,128)S(1)}, f32[1024,512]{1,0:T(8,128)}, u32[]{:S(2)}) copy-start(f32[1024,512]{1,0:T(8,128)} %param.4) | copy-start | bytes 6291460
  18.9 713.4 %reduce-scatter.3.cloned.1.call-start = ((), (), s32[]{:S(2)}) async-start(), calls=%async_computation.2 | async-start | bytes 2129920 | tf_op jit(solution)/shard_map/reduce_scatter | solution.py:85
  18.9 17.2 %collective-permute-start = (f32[128,512]{1,0:T(8,128)S(1)}, f32[128,512]{1,0:T(8,128)S(1)}, u32[]{:S(2)}, u32[]{:S(2)}) collective-permute-start(f32[128,512]{1,0:T(8,128)S(1)} %copy-done.1), channel_id=1, source_target_pairs={{0,1},{1,2},{2,3},{3,4},{4,5},{5,6},{6,7},{7,0},{8,9},{9,10},{10,1... | collective-permute-start | bytes 786440 | tf_op jit(solution)/shard_map/ppermute | solution.py:16
  36.2 16.6 %collective-permute-start.1 = (f32[128,512]{1,0:T(8,128)S(1)}, f32[128,512]{1,0:T(8,128)S(1)}, u32[]{:S(2)}, u32[]{:S(2)}) collective-permute-start(f32[128,512]{1,0:T(8,128)S(1)} %collective-permute-done), channel_id=1, source_target_pairs={{0,1},{1,2},{2,3},{3,4},{4,5},{5,6},{6,7},{7,0},{8,9},{9,10},{10,1... | collective-permute-start | bytes 786440 | tf_op jit(solution)/shard_map/ppermute | solution.py:16
  52.8 16.4 %collective-permute-start.2 = (f32[128,512]{1,0:T(8,128)S(1)}, f32[128,512]{1,0:T(8,128)S(1)}, u32[]{:S(2)}, u32[]{:S(2)}) collective-permute-start(f32[128,512]{1,0:T(8,128)S(1)} %collective-permute-done.1), channel_id=1, source_target_pairs={{0,1},{1,2},{2,3},{3,4},{4,5},{5,6},{6,7},{7,0},{8,9},{9,10},{10,1... | collective-permute-start | bytes 786440 | tf_op jit(solution)/shard_map/ppermute | solution.py:16
  69.1 9.5 %collective-permute-start.3 = (f32[128,512]{1,0:T(8,128)S(1)}, f32[128,512]{1,0:T(8,128)S(1)}, u32[]{:S(2)}, u32[]{:S(2)}) collective-permute-start(f32[128,512]{1,0:T(8,128)S(1)} %collective-permute-done.2), channel_id=1, source_target_pairs={{0,1},{1,2},{2,3},{3,4},{4,5},{5,6},{6,7},{7,0},{8,9},{9,10},{10,1... | collective-permute-start | bytes 786440 | tf_op jit(solution)/shard_map/ppermute | solution.py:16
  78.6 9.5 %collective-permute-start.4 = (f32[128,512]{1,0:T(8,128)S(1)}, f32[128,512]{1,0:T(8,128)S(1)}, u32[]{:S(2)}, u32[]{:S(2)}) collective-permute-start(f32[128,512]{1,0:T(8,128)S(1)} %collective-permute-done.3), channel_id=1, source_target_pairs={{0,1},{1,2},{2,3},{3,4},{4,5},{5,6},{6,7},{7,0},{8,9},{9,10},{10,1... | collective-permute-start | bytes 786440 | tf_op jit(solution)/shard_map/ppermute | solution.py:16
  88.1 9.7 %collective-permute-start.5 = (f32[128,512]{1,0:T(8,128)S(1)}, f32[128,512]{1,0:T(8,128)}, u32[]{:S(2)}, u32[]{:S(2)}) collective-permute-start(f32[128,512]{1,0:T(8,128)S(1)} %collective-permute-done.4), channel_id=1, source_target_pairs={{0,1},{1,2},{2,3},{3,4},{4,5},{5,6},{6,7},{7,0},{8,9},{9,10},{10,1... | collective-permute-start | bytes 786440 | tf_op jit(solution)/shard_map/ppermute | solution.py:16
  97.8 9.8 %collective-permute-start.6 = (f32[128,512]{1,0:T(8,128)}, f32[128,512]{1,0:T(8,128)}, u32[]{:S(2)}, u32[]{:S(2)}) collective-permute-start(f32[128,512]{1,0:T(8,128)} %collective-permute-done.5), channel_id=1, source_target_pairs={{0,1},{1,2},{2,3},{3,4},{4,5},{5,6},{6,7},{7,0},{8,9},{9,10},{10,1... | collective-permute-start | bytes 786440 | tf_op jit(solution)/shard_map/ppermute | solution.py:16
  114.5 8.9 %copy-start.2 = (f32[128,512]{1,0:T(8,128)S(1)}, f32[128,512]{1,0:T(8,128)}, u32[]{:S(2)}) copy-start(f32[128,512]{1,0:T(8,128)} %param.3) | copy-start | bytes 786436
Sparse Core Ops, SparseCore 0:
  19.0 55.6 reduce-scatter.4
  582.2 149.9 reduce-scatter.2
